TPU v7x, 32 devices: a whole 2x2x4 slice. The times are simulated.
32 devices in a mesh: row: 4 (over z), col: 4 (over x, core), depth: 2 (over y).
Axes of the slice: x: 2, y: 2, z: 4, core: 2. Of those that a mesh axis runs over, the one named last changes fastest.
Arguments:
- left_block: bfloat16 [4, 8192, 512], P(None, ('row', 'depth'), 'col'), may hold values from -6 to 6
- right_block: bfloat16 [512, 2, 16384], P(('row', 'depth'), None, 'col'), may hold values from -0.125 to 0.125
- slice_ids: int32 [4], replicated, may hold values from 0 to 1, as said below
- mode_order: int32 [9], replicated, may hold values from 0 to 8, each once
Outputs:
- contracted: float32 [8192, 16384], P(('row', 'depth'), 'col')
Inputs may be any that keep to these rules, and one draw needn't show every extreme that they name: mode_order holds every number of 0 to 8 once. `slice_ids`: each value of the sliced bond is taken by exactly 2 slices.
All inputs are finite; a program needn't handle non-finite values.
Results may differ from a plain program's by a relative error of at most 0.0003.
Values may be sent and summed in bfloat16 or wider, within the bound.
No kernel may reach another device: no remote copies, remote signals or barrier semaphores. Data moves between devices by JAX's collectives and lax.ppermute only.
A program may use at most 128 MiB of HBM per device.

v0:
```python
import jax
import jax.numpy as jnp
from jax import lax
from jax.sharding import PartitionSpec as P


def stored_order(mode_order, columns):
    logical = jnp.arange(columns, dtype=jnp.int32)
    stored = jnp.zeros((columns,), jnp.int32)
    for bit_place in range(mode_order.shape[0]):
        stored = stored + logical // 2**bit_place % 2 * jnp.left_shift(
            jnp.int32(1), mode_order[bit_place]
        )
    return stored


def per_device(left_block, right_block, slice_ids, mode_order):
    values = right_block.shape[1]
    picks = (slice_ids[:, None] == jnp.arange(values, dtype=jnp.int32)[None, :]).astype(jnp.float32)
    folded = jnp.zeros((values,) + left_block.shape[1:], jnp.float32)
    for number in range(left_block.shape[0]):
        folded = (
            folded + picks[number][:, None, None] * left_block[number].astype(jnp.float32)[None]
        )
    whole_left = lax.all_gather(folded, "col", axis=2, tiled=True)
    permuted = jnp.take(whole_left, stored_order(mode_order, whole_left.shape[2]), axis=2)
    return jnp.einsum(
        "crk,kcn->rn",
        permuted,
        lax.all_gather(right_block, ("row", "depth"), axis=0, tiled=True).astype(jnp.float32),
        preferred_element_type=jnp.float32,
        precision=lax.Precision.HIGHEST,
    )


def solution(mesh):
    in_specs = (P(None, ("row", "depth"), "col"), P(("row", "depth"), None, "col"), P(), P())
    out_specs = P(("row", "depth"), "col")
    return jax.shard_map(
        per_device, mesh=mesh, in_specs=in_specs, out_specs=out_specs, check_vma=False
    )
```

profile of v0, /device:TPU:0, one launch (start us, length us, event | category | flops | bytes accessed | tf_op | source)
XLA Modules:
  0.0 218.0 jit_solution(17528352882170684913)
XLA Ops:
  6.5 0.0 all-gather.3.cloned.1.call-start
  6.5 0.7 fusion.70
  7.3 1.3 bitcast_convert_fusion.3
  8.6 0.2 copy.12
  8.8 0.2 copy.13
  9.0 0.2 copy.15
  9.2 0.0 copy-start
  9.2 0.2 copy.14
  9.4 1.9 multiply_add_fusion
  11.3 0.0 all-gather.3.cloned.1.call-update
  11.4 0.0 all-gather.5.cloned.1.call-start
  11.4 2.8 %copy.16 = bf16[64,2,4096]{2,0,1:T(8,128)(2,1)} copy(bf16[64,2,4096]{2,1,0:T(2,128)(2,1)} %param.5) | data formatting | bytes 2097152 | tf_op args[1]
  14.3 0.0 all-gather.5.cloned.1.call-update
  14.3 0.0 copy-done
  14.3 0.7 fusion.71
  20.7 28.0 %all-gather.3.cloned.1.call-done = f32[2,1024,512]{1,0,2:T(2,128)} async-done(((f32[2,1024,128]{1,0,2:T(2,128)}), f32[2,1024,512]{1,0,2:T(2,128)}) %all-gather.3.cloned.1.call-update) | async-done | bytes 4194320 | tf_op jit(solution)/shard_map/all_gather | solution.py:25
  48.7 21.9 %gather_fusion = f32[512,2,1024]{2,1,0:T(2,128)} fusion(f32[2,1024,512]{1,0,2:T(2,128)} %all-gather.3.cloned.1.call-done, s32[1024]{0:T(1024)S(1)} %pad_clamp_fusion), kind=kCustom, calls=%fused_computation | custom fusion | bytes 8390656 | tf_op jit(solution)/shard_map/jit(_take)/gather | solution.py:26
  70.6 6.0 %select_bitcast_fusion = f32[2,1024,512]{1,0,2:T(2,128)} fusion(f32[512,2,1024]{2,1,0:T(2,128)} %gather_fusion, pred[512]{0:T(512)(128)(4,1)S(1)} %compare_and_fusion), kind=kLoop, calls=%fused_computation.3 | loop fusion | flops 1048576 | bytes 8389120 | tf_op jit(solution)/shard_map/jit(_take)/select_n | solution.py:26
  76.6 98.8 %all-gather.5.cloned.1.call-done = bf16[512,2,4096]{2,0,1:T(8,128)(2,1)} async-done(((bf16[64,2,4096]{2,0,1:T(8,128)(2,1)}), bf16[512,2,4096]{2,0,1:T(8,128)(2,1)}) %all-gather.5.cloned.1.call-update) | async-done | bytes 8388624 | tf_op jit(solution)/shard_map/all_gather | solution.py:30
  175.4 35.8 %convolution_bitcast_fusion = f32[1024,4096]{1,0:T(8,128)} fusion(bf16[512,2,4096]{2,0,1:T(8,128)(2,1)} %all-gather.5.cloned.1.call-done, f32[2,1024,512]{1,0,2:T(2,128)} %select_bitcast_fusion), kind=kOutput, calls=%fused_computation.1 | convolution fusion | flops 51539607552 | bytes 29360128 | tf_op jit(solution)/shard_map/crk,kcn->rn/dot_general | solution.py:27
  (4 shorter events, 0.1 us)
Async XLA Ops:
  6.5 42.2 %all-gather.3.cloned.1.call-start = ((), (), s32[]{:S(2)}) async-start(), calls=%async_computation | async-start | bytes 5242880 | tf_op jit(solution)/shard_map/all_gather | solution.py:25
  9.2 5.1 %copy-start = (s32[9]{0:T(128)S(1)}, s32[9]{0:T(128)}, u32[]{:S(2)}) copy-start(s32[9]{0:T(128)} %param.7) | copy-start | bytes 112
  11.4 164.0 %all-gather.5.cloned.1.call-start = ((), (), s32[]{:S(2)}) async-start(), calls=%async_computation.1 | async-start | bytes 9437184 | tf_op jit(solution)/shard_map/all_gather | solution.py:30
Sparse Core Ops, SparseCore 0:
  11.5 37.1 all-gather.2
  50.9 124.4 all-gather.4
where the time goes:
time: 218 us
  waiting for transfers between devices  127 us (58%)
  matrix products  35.8 us (16%)
  local copies, waits for them, and re-layouts  26.2 us (12%)
  between operations  19.1 us (9%)
  other arithmetic  10 us (5%)
    all_gather x1, waiting for transfers between devices, per_device(): lax.all_gather(right_block, ('row', 'depth'), axis=0, tiled=True)  98.8 us
    dot_general x1, matrix products, per_device(): jnp.einsum('crk,kcn->rn', permuted, lax.all_gather(right_block, ('row', '...  35.8 us
    all_gather x1, waiting for transfers between devices, per_device(): whole_left = lax.all_gather(folded, 'col', axis=2, tiled=True)  28 us
    gather x1, local copies, waits for them, and re-layouts, per_device(): jnp.take(whole_left, stored_order(mode_order, whole_left.shape[2]), axis=2)  21.9 us
    select_n x2, other arithmetic, per_device(): jnp.take(whole_left, stored_order(mode_order, whole_left.shape[2]), axis=2)  6.06 us
  transfers between devices with their start and end apart: 2, of which 2 were waited for; matrix products, arithmetic and copies ran while one was open for 14% of the time, Pallas kernels for 0%

commit v1 on v0

--- a/solution.py
+++ b/solution.py
@@ -22,7 +22,12 @@
         folded = (
             folded + picks[number][:, None, None] * left_block[number].astype(jnp.float32)[None]
         )
-    whole_left = lax.all_gather(folded, "col", axis=2, tiled=True)
+    ring = [folded]
+    for hop in range(3):
+        ring.append(lax.ppermute(ring[-1], "col", [(dev, (dev + 1) % 4) for dev in range(4)]))
+    whole_left = jnp.roll(
+        jnp.concatenate(ring[::-1], axis=2), (lax.axis_index("col") + 1) * ring[0].shape[2], axis=2
+    )
     permuted = jnp.take(whole_left, stored_order(mode_order, whole_left.shape[2]), axis=2)
     return jnp.einsum(
         "crk,kcn->rn",

time: 218 us -> 180 us (0.83)
  waiting for transfers between devices: 127 us -> 77.4 us
  local copies, waits for them, and re-layouts: 26.2 us -> 35.4 us
    all_gather x1, waiting for transfers between devices: 98.8 us -> 40.5 us  [per_device(): lax.all_gather(right_block, ('row', 'depth'), axis=0, tiled=True)]
    ppermute x0 -> x3, waiting for transfers between devices: none -> 36.9 us  [per_device(): lax.ppermute(ring[-1], 'col', [(dev, (dev + 1) % 4) for dev in range(4)])]
    all_gather x1 -> x0, waiting for transfers between devices: 28 us -> none  [per_device(): whole_left = lax.all_gather(folded, 'col', axis=2, tiled=True)]
    unnamed x3 -> x11, local copies, waits for them, and re-layouts: 2.85 us -> 8.54 us
    dynamic_slice x0 -> x1, local copies, waits for them, and re-layouts: none -> 3.46 us  [per_device(): jnp.roll(jnp.concatenate(ring[::-1], axis=2), (lax.axis_index('col') + 1)...]
  transfers between devices with their start and end apart: 2 -> 4, of which waited for: 2 -> 4; matrix products, arithmetic and copies ran while one was open for 14% -> 24% of each run, Pallas kernels for 0% -> 0%
where the time goes in v1:
time: 180 us; the launch traced here: 179 us
  waiting for transfers between devices  77.4 us (43%)
  matrix products  35.8 us (20%)
  local copies, waits for them, and re-layouts  35.4 us (20%)
  between operations  19.1 us (11%)
  other arithmetic  11.2 us (6%)
    all_gather x1, waiting for transfers between devices, per_device(): lax.all_gather(right_block, ('row', 'depth'), axis=0, tiled=True)  40.5 us
    ppermute x3, waiting for transfers between devices, per_device(): lax.ppermute(ring[-1], 'col', [(dev, (dev + 1) % 4) for dev in range(4)])  36.9 us
    dot_general x1, matrix products, per_device(): jnp.einsum('crk,kcn->rn', permuted, lax.all_gather(right_block, ('row', '...  35.8 us
    gather x1, local copies, waits for them, and re-layouts, per_device(): jnp.take(whole_left, stored_order(mode_order, whole_left.shape[2]), axis=2)  21.9 us
    unnamed x11, local copies, waits for them, and re-layouts  8.54 us
    select_n x2, other arithmetic, per_device(): jnp.take(whole_left, stored_order(mode_order, whole_left.shape[2]), axis=2)  6.03 us
  transfers between devices with their start and end apart: 4, of which 4 were waited for; matrix products, arithmetic and copies ran while one was open for 24% of the time, Pallas kernels for 0%

profile of v1, /device:TPU:0, one launch (start us, length us, event | category | flops | bytes accessed | tf_op | source)
XLA Modules:
  0.0 179.4 jit_solution(11012731396946883448)
XLA Ops:
  6.5 0.0 all-gather.2.cloned.1.call-start
  6.5 2.9 %copy.10 = bf16[64,2,4096]{2,0,1:T(8,128)(2,1)} copy(bf16[64,2,4096]{2,1,0:T(2,128)(2,1)} %param.5) | data formatting | bytes 2097152 | tf_op args[1]
  9.4 0.0 all-gather.2.cloned.1.call-update
  9.4 1.3 bitcast_convert_fusion.3
  10.8 0.2 copy.6
  11.0 0.2 copy.7
  11.2 0.2 copy.8
  11.4 0.2 copy.9
  11.6 0.0 copy-done.1
  11.6 0.1 fusion.70
  11.7 1.1 multiply_add_fusion
  12.8 0.5 collective-permute-start
  13.3 14.4 %collective-permute-done = f32[2,1024,128]{1,0,2:T(2,128)S(1)} collective-permute-done((f32[2,1024,128]{1,0,2:T(2,128)S(1)}, f32[2,1024,128]{1,0,2:T(2,128)S(1)}, u32[]{:S(2)}, u32[]{:S(2)}) %collective-permute-start) | collective-permute-done | bytes 1048608 | tf_op jit(solution)/shard_map/ppermute | solution.py:27
  27.7 0.0 collective-permute-start.1
  27.7 14.3 %collective-permute-done.1 = f32[2,1024,128]{1,0,2:T(2,128)} collective-permute-done((f32[2,1024,128]{1,0,2:T(2,128)S(1)}, f32[2,1024,128]{1,0,2:T(2,128)}, u32[]{:S(2)}, u32[]{:S(2)}) %collective-permute-start.1) | collective-permute-done | bytes 1048608 | tf_op jit(solution)/shard_map/ppermute | solution.py:27
  42.1 0.0 collective-permute-start.2
  42.1 0.0 copy-done
  42.1 0.7 fusion.71
  48.4 8.2 %collective-permute-done.2 = f32[2,1024,128]{1,0,2:T(2,128)} collective-permute-done((f32[2,1024,128]{1,0,2:T(2,128)}, f32[2,1024,128]{1,0,2:T(2,128)}, u32[]{:S(2)}, u32[]{:S(2)}) %collective-permute-start.2) | collective-permute-done | bytes 1048608 | tf_op jit(solution)/shard_map/ppermute | solution.py:27
  56.6 1.3 constant_dynamic-update-slice_fusion.7
  57.9 1.4 constant_dynamic-update-slice_fusion.6
  59.3 0.1 constant_dynamic-update-slice_fusion.5
  59.4 1.4 constant_dynamic-update-slice_fusion.4
  60.8 1.4 constant_dynamic-update-slice_fusion.3
  62.2 1.4 constant_dynamic-update-slice_fusion.2
  63.6 0.1 constant_dynamic-update-slice_fusion.1
  63.7 1.2 constant_dynamic-update-slice_fusion
  64.9 3.5 %constant_dynamic-slice_fusion = f32[2,1024,512]{1,0,2:T(2,128)} fusion(f32[2,1024,1024]{1,0,2:T(2,128)S(1)} %constant_dynamic-update-slice_fusion, s32[]{:T(128)S(6)} %select_n.306), kind=kLoop, calls=%fused_computation.195 | loop fusion | bytes 8388612 | tf_op jit(solution)/shard_map/jit(_roll_dynamic)/dynamic_slice | solution.py:28
  68.4 21.9 %gather_fusion = f32[512,2,1024]{2,1,0:T(2,128)} fusion(f32[2,1024,512]{1,0,2:T(2,128)} %constant_dynamic-slice_fusion, s32[1024]{0:T(1024)S(1)} %pad_clamp_fusion), kind=kCustom, calls=%fused_computation | custom fusion | bytes 8390656 | tf_op jit(solution)/shard_map/jit(_take)/gather | solution.py:31
  90.3 6.0 %select_bitcast_fusion = f32[2,1024,512]{1,0,2:T(2,128)} fusion(f32[512,2,1024]{2,1,0:T(2,128)} %gather_fusion, pred[512]{0:T(512)(128)(4,1)S(1)} %compare_and_fusion), kind=kLoop, calls=%fused_computation.3 | loop fusion | flops 1048576 | bytes 8389120 | tf_op jit(solution)/shard_map/jit(_take)/select_n | solution.py:31
  96.3 40.5 %all-gather.2.cloned.1.call-done = bf16[512,2,4096]{2,0,1:T(8,128)(2,1)} async-done(((bf16[64,2,4096]{2,0,1:T(8,128)(2,1)}), bf16[512,2,4096]{2,0,1:T(8,128)(2,1)}) %all-gather.2.cloned.1.call-update) | async-done | bytes 8388624 | tf_op jit(solution)/shard_map/all_gather | solution.py:35
  136.8 35.8 %convolution_bitcast_fusion = f32[1024,4096]{1,0:T(8,128)} fusion(bf16[512,2,4096]{2,0,1:T(8,128)(2,1)} %all-gather.2.cloned.1.call-done, f32[2,1024,512]{1,0,2:T(2,128)} %select_bitcast_fusion), kind=kOutput, calls=%fused_computation.1 | convolution fusion | flops 51539607552 | bytes 29360128 | tf_op jit(solution)/shard_map/crk,kcn->rn/dot_general | solution.py:32
  (6 shorter events, 0.1 us)
Async XLA Ops:
  6.5 5.1 %copy-start.1 = (s32[4]{0:T(128)S(1)}, s32[4]{0:T(128)}, u32[]{:S(2)}) copy-start(s32[4]{0:T(128)} %param.6) | copy-start | bytes 52
  6.5 35.5 %copy-start = (s32[9]{0:T(128)S(1)}, s32[9]{0:T(128)}, u32[]{:S(2)}) copy-start(s32[9]{0:T(128)} %param.7) | copy-start | bytes 112
  6.5 130.2 %all-gather.2.cloned.1.call-start = ((), (), s32[]{:S(2)}) async-start(), calls=%async_computation | async-start | bytes 9437184 | tf_op jit(solution)/shard_map/all_gather | solution.py:35
  12.8 14.9 %collective-permute-start = (f32[2,1024,128]{1,0,2:T(2,128)S(1)}, f32[2,1024,128]{1,0,2:T(2,128)S(1)}, u32[]{:S(2)}, u32[]{:S(2)}) collective-permute-start(f32[2,1024,128]{1,0,2:T(2,128)S(1)} %multiply_add_fusion), channel_id=1, source_target_pairs={{0,2},{2,4},{4,6},{6,0},{1,3},{3,5},{5,7},{7,1},{8,10},{10,12},{12... | collective-permute-start | bytes 3145736 | tf_op jit(solution)/shard_map/ppermute | solution.py:27
  27.7 14.3 %collective-permute-start.1 = (f32[2,1024,128]{1,0,2:T(2,128)S(1)}, f32[2,1024,128]{1,0,2:T(2,128)}, u32[]{:S(2)}, u32[]{:S(2)}) collective-permute-start(f32[2,1024,128]{1,0,2:T(2,128)S(1)} %collective-permute-done), channel_id=1, source_target_pairs={{0,2},{2,4},{4,6},{6,0},{1,3},{3,5},{5,7},{7,1},{8,10},{10,12},{12... | collective-permute-start | bytes 3145736 | tf_op jit(solution)/shard_map/ppermute | solution.py:27
  42.1 14.5 %collective-permute-start.2 = (f32[2,1024,128]{1,0,2:T(2,128)}, f32[2,1024,128]{1,0,2:T(2,128)}, u32[]{:S(2)}, u32[]{:S(2)}) collective-permute-start(f32[2,1024,128]{1,0,2:T(2,128)} %collective-permute-done.1), channel_id=1, source_target_pairs={{0,2},{2,4},{4,6},{6,0},{1,3},{3,5},{5,7},{7,1},{8,10},{10,12},{12... | collective-permute-start | bytes 3145736 | tf_op jit(solution)/shard_map/ppermute | solution.py:27
Sparse Core Ops, SparseCore 0:
  9.6 127.1 all-gather.1
